TPU v7x, 32 devices: a whole 2x2x4 slice. The times are simulated.
32 devices in a mesh: section: 4 (over z), dp: 4 (over x, core), mp: 2 (over y).
Axes of the slice: x: 2, y: 2, z: 4, core: 2. Of those that a mesh axis runs over, the one named last changes fastest.
Arguments:
- hidden: bfloat16 [4, 16, 4, 4096], P('section', 'mp', 'dp'), may hold values from -2048 to 2048
- token_ids: int32 [16, 4], P('mp', 'dp'), may hold values from 0 to 8191
- seq_lengths: int32 [4], replicated, may hold values from 1 to 16, 21 in all
- head_slices: bfloat16 [4, 4096, 8192], P('section', None, ('dp', 'mp')), may hold values from -8 to 8
- value_head: bfloat16 [4, 4096], P('section'), may hold values from -0.09375 to 0.09375
Outputs:
- scores: float32 [4, 16, 4], P('section', 'mp', 'dp')
- advantages: float32 [16, 4], P('mp', 'dp')
- trunk_grad: bfloat16 [4, 16, 4, 4096], P('section', 'mp', 'dp')
Inputs may be any that keep to these rules, and one draw needn't show every extreme that they name: Sequence j is live at positions 0 to seq_lengths[j] - 1; the lengths sum to 21 and one of them is 16.
All inputs are finite; a program needn't handle non-finite values.
Results may differ from a plain program's by a relative error of at most 0.0047.
Values may be sent and summed in bfloat16 or wider, within the bound.
A program may use at most 64 MiB of HBM per device.

v0:
```python
import math
import jax
import jax.numpy as jnp
from jax import lax
from jax.sharding import PartitionSpec as P

gae_decay = 0.95
reward_gain = 0.5
drift_gain = 0.1
penalty_gain = 0.2
loss_scale = 16.0


def from_root(value, axis, source):
    kept = jnp.where(lax.axis_index(axis) == source, value, 0).astype(value.dtype)
    return lax.psum(kept, axis)


def joined(x, axis, combine):
    everything = jax.tree.map(lambda part: lax.all_gather(part, axis), x)
    first = jax.tree.map(lambda part: part[0], everything)

    def turn(k, so_far):
        return combine(so_far, jax.tree.map(lambda part: part[k], everything))

    return lax.fori_loop(1, lax.axis_size(axis), turn, first)


def block_logits(gathered, head_part):
    return jnp.dot(gathered, head_part, preferred_element_type=jnp.float32)


def merge_parts(earlier_part, later_part):
    maximum = jnp.maximum(earlier_part[0], later_part[0])
    exp_total = earlier_part[1] * jnp.exp(earlier_part[0] - maximum) + later_part[1] * jnp.exp(
        later_part[0] - maximum
    )
    return (maximum, exp_total, earlier_part[2] + later_part[2])


def local(hidden, token_ids, seq_lengths, head_slices, value_head):
    sections = lax.axis_size("section")
    per_device = hidden.shape[1]
    model_width = hidden.shape[3]
    vocab_part = head_slices.shape[2]
    seq_count = seq_lengths.shape[0]
    length = per_device * lax.axis_size("mp")
    head_part = head_slices[0]
    critic_head = value_head[0]
    own_block = from_root(hidden, "section", 0)
    gathered, row_ids = (
        lax.all_gather(own_block[0, :, 0, :], ("dp", "mp"), axis=0, tiled=True),
        lax.all_gather(token_ids[:, 0], ("dp", "mp"), axis=0, tiled=True),
    )
    row_total = gathered.shape[0]
    row_iota = lax.broadcasted_iota(jnp.int32, (row_total,), 0)
    seq_of = row_iota // length
    pos_of = row_iota % length
    seq_table = lax.broadcasted_iota(jnp.int32, (row_total, seq_count), 1)
    length_of = jnp.sum(jnp.where(seq_of[:, None] == seq_table, seq_lengths[None, :], 0), axis=1)
    live_bool = pos_of < length_of
    live_mask = live_bool.astype(jnp.float32)
    logits = block_logits(gathered, head_part)
    own_index = lax.axis_index("dp") * lax.axis_size("mp") + lax.axis_index("mp")
    vocab_start = own_index * vocab_part
    column = lax.broadcasted_iota(jnp.int32, logits.shape, 1) + vocab_start
    maximum = jnp.max(logits, axis=1)
    exp_total = jnp.sum(jnp.exp(logits - maximum[:, None]), axis=1)
    picked = jnp.sum(jnp.where(column == row_ids[:, None], logits, jnp.float32(0.0)), axis=1)
    values = jnp.dot(gathered, critic_head, preferred_element_type=jnp.float32)
    maximum, exp_total, picked = joined((maximum, exp_total, picked), ("dp", "mp"), merge_parts)
    normal = maximum + jnp.log(exp_total)
    scored = jnp.where(live_bool, picked - normal, jnp.float32(0.0))
    own_start = own_index * per_device
    scores_out = lax.dynamic_slice_in_dim(scored, own_start, per_device, 0).reshape(
        1, per_device, 1
    )
    joined_scores, joined_values = (
        lax.all_gather(scored[None, :], "section", axis=0, tiled=True),
        lax.all_gather(values[None, :], "section", axis=0, tiled=True),
    )
    behaviour = joined_scores[0]
    implicit = joined_scores[1]
    anchor = joined_scores[2]
    current = joined_scores[3]
    reward = (reward_gain * (implicit - anchor) - drift_gain * (behaviour - anchor)).reshape(
        seq_count, length
    )
    critic_grid = joined_values[1].reshape(seq_count, length)
    live_grid = live_mask.reshape(seq_count, length)
    next_values = jnp.concatenate(
        [critic_grid[:, 1:], jnp.zeros((seq_count, 1), jnp.float32)], axis=1
    )
    next_mask = jnp.concatenate([live_grid[:, 1:], jnp.zeros((seq_count, 1), jnp.float32)], axis=1)
    td_error = live_grid * (reward + next_mask * next_values - critic_grid)
    later_pos = lax.broadcasted_iota(jnp.int32, (length, length), 0)
    earlier = lax.broadcasted_iota(jnp.int32, (length, length), 1)
    weights_t = jnp.where(
        later_pos >= earlier,
        jnp.exp((later_pos - earlier).astype(jnp.float32) * math.log(gae_decay)),
        jnp.float32(0.0),
    )
    advantage = jnp.dot(td_error, weights_t, precision=lax.Precision.HIGHEST).reshape(row_total)
    advantage_out = lax.dynamic_slice_in_dim(advantage, own_start, per_device, 0).reshape(
        per_device, 1
    )
    prob_ratio = jnp.exp(current - behaviour)
    token_grad = (
        -(loss_scale / seq_count)
        * live_mask
        * (prob_ratio * advantage - penalty_gain * (prob_ratio - 1.0))
    )
    soft_probs = jnp.exp(logits - normal[:, None])
    target_hit = (column == row_ids[:, None]).astype(jnp.float32)
    slope = (token_grad[:, None] * (target_hit - soft_probs)).astype(jnp.bfloat16)
    grad_rows = lax.psum_scatter(
        lax.dot_general(
            slope, head_part, (((1,), (1,)), ((), ())), preferred_element_type=jnp.float32
        ),
        ("dp", "mp"),
        scatter_dimension=0,
        tiled=True,
    )
    learner = (lax.axis_index("section") == sections - 1).astype(jnp.float32)
    trunk_out = (grad_rows * learner).astype(jnp.bfloat16).reshape(1, per_device, 1, model_width)
    return (scores_out, advantage_out, trunk_out)


def solution(mesh):
    return jax.shard_map(
        local,
        mesh=mesh,
        in_specs=(
            P("section", "mp", "dp", None),
            P("mp", "dp"),
            P(),
            P("section", None, ("dp", "mp")),
            P("section", None),
        ),
        out_specs=(P("section", "mp", "dp"), P("mp", "dp"), P("section", "mp", "dp", None)),
        check_vma=False,
    )
```

profile of v0, /device:TPU:0, one launch (start us, length us, event | category | flops | bytes accessed | tf_op | source)
XLA Modules:
  0.0 146.0 jit_solution(6107833239940460607)
XLA Ops:
  7.2 1.5 %select_bitcast_fusion = bf16[8,4096]{1,0:T(8,128)(2,1)} fusion(bf16[1,8,1,4096]{3,1,2,0:T(8,128)(2,1)} %param.7, pred[]{:T(512)S(6)} %eq.30), kind=kLoop, calls=%fused_computation.28 | loop fusion | flops 32768 | bytes 131073 | tf_op jit(solution)/shard_map/squeeze | solution.py:52
  8.8 1.2 dynamic-slice.4
  10.1 1.2 dynamic-slice
  13.2 0.8 bitcast_dynamic-update-slice_fusion
  14.0 8.8 %all-reduce.4 = s32[64]{0:T(128)S(1)} all-reduce(s32[64]{0:T(128)S(1)} %bitcast_dynamic-update-slice_fusion), channel_id=4, replica_groups=mesh['section'=4,'dp'=4,'mp'=2] {'dp','mp'}, use_global_device_ids=true, to_apply=%add.4 | all-reduce | flops 64 | bytes 512
  22.8 0.7 select_reduce_fusion
  23.7 24.2 %all-reduce.12.cloned.1.call-done = bf16[8,4096]{1,0:T(8,128)(2,1)} async-done(((bf16[8,4096]{1,0:T(8,128)(2,1)}), bf16[8,4096]{1,0:T(8,128)(2,1)}) %all-reduce.12.cloned.1.call-update) | async-done | bytes 65552 | tf_op jit(solution)/shard_map/psum | solution.py:16
  47.9 16.6 %all_gather.30 = bf16[64,4096]{1,0:T(8,128)(2,1)S(1)} all-gather(bf16[8,4096]{1,0:T(8,128)(2,1)} %all-reduce.12.cloned.1.call-done), channel_id=1, replica_groups=mesh['section'=4,'dp'=4,'mp'=2] {'dp','mp'}, dimensions={0}, use_global_device_ids=true | all-gather | bytes 589824 | tf_op jit(solution)/shard_map/all_gather | solution.py:52
  64.5 5.1 %fusion.45 = (f32[64]{0:T(128)S(1)}, f32[64,1024]{1,0:T(8,128)S(1)}) fusion(bf16[64,4096]{1,0:T(8,128)(2,1)S(1)} %all_gather.30, bf16[1,4096,1024]{2,1,0:T(8,128)(2,1)} %param.10), kind=kOutput, calls=%fused_computation.72 | convolution fusion | flops 536936384 | bytes 9175296 | tf_op jit(solution)/shard_map/dot_general | solution.py:30
  69.5 0.2 dynamic-update-slice
  69.8 0.2 fusion.11
  70.0 0.2 dynamic-update-slice.3
  70.3 0.2 dynamic-update-slice.1
  70.5 14.3 %all-reduce.8 = (f32[512]{0:T(512)S(1)}, f32[512]{0:T(512)S(1)}, f32[512]{0:T(512)S(1)}) all-reduce(f32[512]{0:T(512)S(1)} %dynamic-update-slice, f32[512]{0:T(512)S(1)} %dynamic-update-slice.1, f32[512]{0:T(512)S(1)} %dynamic-update-slice.3), channel_id=2, replica_groups=mesh['section'=4,'dp'=4,'mp'=2] {'dp','mp'}, use_global_device_ids=true, to_apply=%add.2 | all-reduce | flops 1536 | bytes 12288
  85.0 0.2 convolution_bitcast_fusion
  85.2 0.3 while.19
  85.5 0.2 dynamic-update-slice.5
  85.9 10.4 %all-reduce.9 = (f32[256]{0:T(256)S(1)}, f32[256]{0:T(256)S(1)}) all-reduce(f32[256]{0:T(256)S(1)} %dynamic-update-slice.5, f32[256]{0:T(256)S(1)} %get-tuple-element.207), channel_id=7, replica_groups=mesh['section'=4,'dp'=4,'mp'=2] {'section'}, use_global_device_ids=true, to_apply=%add.7 | all-reduce | flops 512 | bytes 4096
  96.7 0.1 fusion.26
  97.0 7.1 %fusion.7 = f32[64,4096]{1,0:T(8,128)} fusion(bf16[1,4096,1024]{2,1,0:T(8,128)(2,1)} %param.10, f32[64,1024]{1,0:T(8,128)S(1)} %get-tuple-element.212, f32[64]{0:T(128)S(1)} %get-tuple-element.209, f32[64]{0:T(128)S(1)} %subtract_multiply_fusion, s32[1024]{0:T(1024)S(1)} %iota_add_fusion, s32[64]{0:T(128)S(1)} %all-reduce.4), kind=kOutput, calls=%fused_computation.10 | convolution fusion | flops 537264128 | bytes 9704192 | tf_op jit(solution)/shard_map/dot_general | solution.py:117
  104.1 0.6 dynamic-slice_bitcast_fusion
  104.7 0.6 dynamic-slice_bitcast_fusion.1
  105.3 32.4 %reduce-scatter.2.cloned.1.call-done = f32[8,4096]{1,0:T(8,128)} async-done(((f32[64,4096]{1,0:T(8,128)}), f32[8,4096]{1,0:T(8,128)}) %reduce-scatter.2.cloned.1.call-update) | async-done | bytes 131088 | tf_op jit(solution)/shard_map/reduce_scatter | solution.py:116
  137.7 1.5 %fusion.20 = bf16[1,8,1,4096]{3,1,2,0:T(8,128)(2,1)} fusion(f32[8,4096]{1,0:T(8,128)} %reduce-scatter.2.cloned.1.call-done, f32[]{:T(128)S(6)} %convert_element_type.22), kind=kLoop, calls=%fused_computation.27 | loop fusion | flops 65536 | bytes 196612 | tf_op jit(solution)/shard_map/reshape | solution.py:125
  (38 shorter events, 1.4 us)
Async XLA Ops:
  7.2 77.8 %copy-start = (bf16[1,4096]{1,0:T(2,128)(2,1)S(1)}, bf16[1,4096]{1,0:T(2,128)(2,1)}, u32[]{:S(2)}) copy-start(bf16[1,4096]{1,0:T(2,128)(2,1)} %param.11) | copy-start | bytes 24580
  7.2 40.7 %all-reduce.12.cloned.1.call-start = ((), (), s32[]{:S(2)}) async-start(), calls=%async_computation.1 | async-start | bytes 131072 | tf_op jit(solution)/shard_map/psum | solution.py:16
  8.7 128.9 %reduce-scatter.2.cloned.1.call-start = ((), (), s32[]{:S(2)}) async-start(), calls=%async_computation.2 | async-start | bytes 1179648 | tf_op jit(solution)/shard_map/reduce_scatter | solution.py:116
Sparse Core Ops, SparseCore 0:
  10.9 37.0 all-reduce.11
  104.2 33.4 reduce-scatter.1
where the time goes:
time: 146 us
  waiting for transfers between devices  56.6 us (39%)
  blocking collectives  50.1 us (34%)
  between operations  16 us (11%)
  matrix products  12.5 us (9%)
  local copies, waits for them, and re-layouts  6.16 us (4%)
  other arithmetic  4.46 us (3%)
    unnamed x3, blocking collectives  33.5 us
    reduce_scatter x1, waiting for transfers between devices, local(): lax.psum_scatter(lax.dot_general(slope, head_part, (((1,), (1,)), ((), ()...  32.4 us
    psum x1, waiting for transfers between devices, from_root(): return lax.psum(kept, axis)  24.2 us
    all_gather x1, blocking collectives, local(): lax.all_gather(own_block[0, :, 0, :], ('dp', 'mp'), axis=0, tiled=True)  16.6 us
    dot_general x1, matrix products, local(): lax.dot_general(slope, head_part, (((1,), (1,)), ((), ())), preferred_ele...  7.06 us
    dot_general x1, matrix products, block_logits(): return jnp.dot(gathered, head_part, preferred_element_type=jnp.float32)  5.06 us
    unnamed x14, local copies, waits for them, and re-layouts  4.19 us
  transfers between devices with their start and end apart: 2, of which 2 were waited for; matrix products, arithmetic and copies ran while one was open for 4% of the time, Pallas kernels for 0%

commit v1 on v0

--- a/solution.py
+++ b/solution.py
@@ -13,7 +13,11 @@
 
 def from_root(value, axis, source):
     kept = jnp.where(lax.axis_index(axis) == source, value, 0).astype(value.dtype)
-    return lax.psum(kept, axis)
+
+    def obtain_arrays(target):
+        return lax.all_gather(target, axis).sum(axis=0)
+
+    return obtain_arrays(kept)
 
 
 def joined(x, axis, combine):

time: 146 us -> 135 us (0.925)
  waiting for transfers between devices: 56.6 us -> 31.9 us
  blocking collectives: 50.1 us -> 64.9 us
    psum x1 -> x0, waiting for transfers between devices: 24.2 us -> none  [from_root(): return lax.psum(kept, axis)]
    all_gather x0 -> x1, blocking collectives: none -> 13.9 us  [obtain_arrays(): return lax.all_gather(target, axis).sum(axis=0)]
    squeeze x1 -> x0, other arithmetic: 1.48 us -> none  [local(): own_block[0, :, 0, :]]
    unnamed x14 -> x18, local copies, waits for them, and re-layouts: 4.19 us -> 3.54 us
  transfers between devices with their start and end apart: 2 -> 1, of which waited for: 2 -> 1; matrix products, arithmetic and copies ran while one was open for 4% -> 1% of each run, Pallas kernels for 0% -> 0%
where the time goes in v1:
time: 135 us; the launch traced here: 134 us
  blocking collectives  64.9 us (48%)
  waiting for transfers between devices  31.9 us (24%)
  between operations  16.1 us (12%)
  matrix products  12.5 us (9%)
  local copies, waits for them, and re-layouts  5.5 us (4%)
  other arithmetic  3.21 us (2%)
    unnamed x3, blocking collectives  34.4 us
    reduce_scatter x1, waiting for transfers between devices, local(): lax.psum_scatter(lax.dot_general(slope, head_part, (((1,), (1,)), ((), ()...  31.9 us
    all_gather x1, blocking collectives, local(): lax.all_gather(own_block[0, :, 0, :], ('dp', 'mp'), axis=0, tiled=True)  16.6 us
    all_gather x1, blocking collectives, obtain_arrays(): return lax.all_gather(target, axis).sum(axis=0)  13.9 us
    dot_general x1, matrix products, local(): lax.dot_general(slope, head_part, (((1,), (1,)), ((), ())), preferred_ele...  7.06 us
    dot_general x1, matrix products, block_logits(): return jnp.dot(gathered, head_part, preferred_element_type=jnp.float32)  5.08 us
    unnamed x18, local copies, waits for them, and re-layouts  3.54 us
  transfers between devices with their start and end apart: 1, of which 1 were waited for; matrix products, arithmetic and copies ran while one was open for 1% of the time, Pallas kernels for 0%

profile of v1, /device:TPU:0, one launch (start us, length us, event | category | flops | bytes accessed | tf_op | source)
XLA Modules:
  0.0 134.3 jit_solution(10524788118377774686)
XLA Ops:
  7.3 1.2 dynamic-slice
  9.8 0.8 bitcast_dynamic-update-slice_fusion
  10.6 8.8 %all-reduce.4 = s32[64]{0:T(128)S(1)} all-reduce(s32[64]{0:T(128)S(1)} %bitcast_dynamic-update-slice_fusion), channel_id=5, replica_groups=mesh['section'=4,'dp'=4,'mp'=2] {'dp','mp'}, use_global_device_ids=true, to_apply=%add.4 | all-reduce | flops 64 | bytes 512
  19.4 0.8 broadcast_select_fusion
  20.2 13.9 %all-gather = bf16[4,8,1,4096]{3,1,2,0:T(8,128)(2,1)S(1)} all-gather(bf16[1,8,1,4096]{3,1,2,0:T(8,128)(2,1)S(1)} %broadcast_select_fusion), channel_id=2, replica_groups=mesh['section'=4,'dp'=4,'mp'=2] {'section'}, dimensions={0}, use_global_device_ids=true | all-gather | bytes 327680 | tf_op jit(solution)/shard_map/all_gather | solution.py:18
  34.2 16.6 %all_gather.38 = bf16[64,4096]{1,0:T(8,128)(2,1)S(1)} all-gather(bf16[8,4096]{1,0:T(8,128)(2,1)S(1)} %reduce.2), channel_id=1, replica_groups=mesh['section'=4,'dp'=4,'mp'=2] {'dp','mp'}, dimensions={0}, use_global_device_ids=true | all-gather | bytes 589824 | tf_op jit(solution)/shard_map/all_gather | solution.py:56
  50.8 5.1 %fusion.45 = (f32[64]{0:T(128)S(1)}, f32[64,1024]{1,0:T(8,128)S(1)}) fusion(bf16[64,4096]{1,0:T(8,128)(2,1)S(1)} %all_gather.38, bf16[1,4096,1024]{2,1,0:T(8,128)(2,1)} %param.10), kind=kOutput, calls=%fused_computation.72 | convolution fusion | flops 536936384 | bytes 9175296 | tf_op jit(solution)/shard_map/dot_general | solution.py:34
  55.9 0.2 dynamic-update-slice
  56.2 0.2 fusion.11
  56.4 0.2 dynamic-update-slice.3
  56.6 0.2 dynamic-update-slice.1
  56.8 14.1 %all-reduce.8 = (f32[512]{0:T(512)S(1)}, f32[512]{0:T(512)S(1)}, f32[512]{0:T(512)S(1)}) all-reduce(f32[512]{0:T(512)S(1)} %dynamic-update-slice, f32[512]{0:T(512)S(1)} %dynamic-update-slice.1, f32[512]{0:T(512)S(1)} %dynamic-update-slice.3), channel_id=3, replica_groups=mesh['section'=4,'dp'=4,'mp'=2] {'dp','mp'}, use_global_device_ids=true, to_apply=%add.2 | all-reduce | flops 1536 | bytes 12288
  71.2 0.6 dynamic-slice.4
  72.7 0.2 convolution_bitcast_fusion
  73.0 0.3 while.19
  73.3 0.2 dynamic-update-slice.5
  73.5 0.1 fusion.44
  73.6 11.4 %all-reduce.9 = (f32[256]{0:T(256)S(1)}, f32[256]{0:T(256)S(1)}) all-reduce(f32[256]{0:T(256)S(1)} %dynamic-update-slice.5, f32[256]{0:T(256)S(1)} %get-tuple-element.207), channel_id=8, replica_groups=mesh['section'=4,'dp'=4,'mp'=2] {'section'}, use_global_device_ids=true, to_apply=%add.7 | all-reduce | flops 512 | bytes 4096
  85.5 0.1 fusion.26
  85.8 7.1 %fusion.7 = f32[64,4096]{1,0:T(8,128)} fusion(bf16[1,4096,1024]{2,1,0:T(8,128)(2,1)} %param.10, f32[64,1024]{1,0:T(8,128)S(1)} %get-tuple-element.212, f32[64]{0:T(128)S(1)} %get-tuple-element.209, f32[64]{0:T(128)S(1)} %subtract_multiply_fusion, s32[1024]{0:T(1024)S(1)} %iota_add_fusion, s32[64]{0:T(128)S(1)} %all-reduce.4), kind=kOutput, calls=%fused_computation.10 | convolution fusion | flops 537264128 | bytes 9704192 | tf_op jit(solution)/shard_map/dot_general | solution.py:121
  92.9 0.6 dynamic-slice_bitcast_fusion
  93.4 0.6 dynamic-slice_bitcast_fusion.1
  94.0 31.9 %reduce-scatter.2.cloned.1.call-done = f32[8,4096]{1,0:T(8,128)} async-done(((f32[64,4096]{1,0:T(8,128)}), f32[8,4096]{1,0:T(8,128)}) %reduce-scatter.2.cloned.1.call-update) | async-done | bytes 131088 | tf_op jit(solution)/shard_map/reduce_scatter | solution.py:120
  125.9 1.5 %fusion.20 = bf16[1,8,1,4096]{3,1,2,0:T(8,128)(2,1)} fusion(f32[8,4096]{1,0:T(8,128)} %reduce-scatter.2.cloned.1.call-done, f32[]{:T(128)S(6)} %convert_element_type.24), kind=kLoop, calls=%fused_computation.27 | loop fusion | flops 65536 | bytes 196612 | tf_op jit(solution)/shard_map/reshape | solution.py:129
  (41 shorter events, 1.4 us)
Async XLA Ops:
  7.2 65.6 %copy-start = (bf16[1,4096]{1,0:T(2,128)(2,1)S(1)}, bf16[1,4096]{1,0:T(2,128)(2,1)}, u32[]{:S(2)}) copy-start(bf16[1,4096]{1,0:T(2,128)(2,1)} %param.11) | copy-start | bytes 24580
  7.2 118.7 %reduce-scatter.2.cloned.1.call-start = ((), (), s32[]{:S(2)}) async-start(), calls=%async_computation.1 | async-start | bytes 1179648 | tf_op jit(solution)/shard_map/reduce_scatter | solution.py:120
  50.8 20.4 %copy-start.2 = (u32[32]{0:T(128)S(1)}, u32[32]{0:T(128)}, u32[]{:S(2)}) copy-start(u32[32]{0:T(128)} %constant.151) | copy-start | bytes 388
  50.8 21.6 %copy-start.1 = (s32[4]{0:T(128)S(1)}, s32[4]{0:T(128)}, u32[]{:S(2)}) copy-start(s32[4]{0:T(128)} %param.9) | copy-start | bytes 52
Sparse Core Ops, SparseCore 0:
  93.0 32.8 reduce-scatter.1
